TPU v7x, 32 devices: a whole 2x2x4 slice. The times are simulated.
32 devices in a mesh: pair: 32 (over z, y, x, core), aux: 1.
Axes of the slice: x: 2, y: 2, z: 4, core: 2. Of those that a mesh axis runs over, the one named last changes fastest.
Arguments:
- amplitudes: bfloat16 [256, 512, 512], P(None, 'pair'), may hold values from -6 to 6
- ladder: bfloat16 [256, 256], replicated, may hold values from -0.375 to 0.375
- cholesky: bfloat16 [8, 512, 512], P('aux'), may hold values from -0.25 to 0.25
- pair_ids: int32 [256], P('pair'), may hold values from 0 to 255, each once
- occ_energy: float32 [16], replicated, may hold values from -2 to -0.5
- vir_energy: float32 [512], replicated, may hold values from 0.5 to 3
Outputs:
- update: float32 [256, 512, 512], P('pair', None, 'aux')
Inputs may be any that keep to these rules, and one draw needn't show every extreme that they name: `pair_ids`: every value 0 to 255 appears once.
All inputs are finite; a program needn't handle non-finite values.
Results may differ from a plain program's by a relative error of at most 0.0029.
Values may be sent and summed in bfloat16 or wider, within the bound.
A program may use at most 128 MiB of HBM per device.

v0:
```python
import functools

import jax
import jax.numpy as jnp
from jax import lax
from jax.experimental import pallas as pl
from jax.experimental.pallas import tpu as pltpu
from jax.sharding import PartitionSpec as P

NO = 16
MESH = pl.DeviceIdType.MESH


def residual_kernel(
    n, amps, ladder, chol, pair_ids, occ, vir, out, own_hole,
    amp_own, wide, ladder_v, chol_v, amp_all, hole_all, vir_sum, vir_v, result, ids_s, occ_s,
    amp_send, amp_recv, hole_send, hole_recv, local_sem, out_sem,
):
    total, rows, width = amps.shape
    pairs = total // n
    full = rows * n
    n_vec = chol.shape[0]
    me = lax.axis_index("pair")
    half, quarter = n // 2, n // 4
    order = [a + b for a in range(quarter) for b in (half + quarter, half, quarter, 0) if a + b]
    mine = pl.ds(pl.multiple_of(me * rows, rows), rows)
    own_pairs = pl.ds(me * pairs, pairs)

    load_amp = pltpu.make_async_copy(amps, amp_own, local_sem.at[0])
    load_ladder = pltpu.make_async_copy(ladder, ladder_v, local_sem.at[1])
    load_chol = pltpu.make_async_copy(chol, chol_v, local_sem.at[2])
    keep_amp = pltpu.make_async_copy(amps.at[own_pairs], amp_all.at[:, mine], local_sem.at[3])
    load_ids = pltpu.make_async_copy(pair_ids, ids_s, local_sem.at[4])
    load_occ = pltpu.make_async_copy(occ, occ_s, local_sem.at[5])
    load_vir = pltpu.make_async_copy(vir, vir_v, local_sem.at[6])

    barrier = pltpu.get_barrier_semaphore()
    for k in range(1, n):
        pl.semaphore_signal(barrier, inc=1, device_id={"pair": me ^ k}, device_id_type=MESH)
    pl.semaphore_wait(barrier, n - 1)

    amp_copies = []
    for k in order:
        dest = me ^ k
        copy = pltpu.make_async_remote_copy(
            amps.at[pl.ds(dest * pairs, pairs)], amp_all.at[:, mine],
            amp_send.at[k], amp_recv.at[k], device_id={"pair": dest}, device_id_type=MESH,
        )
        copy.start()
        amp_copies.append(copy)
    load_amp.start()
    load_ladder.start()
    load_chol.start()
    keep_amp.start()
    load_ids.start()
    load_occ.start()
    load_vir.start()

    load_amp.wait()
    load_ladder.wait()
    block = 16
    lanes = 128

    def columns(j, carry):
        cols = pl.ds(pl.multiple_of(j * lanes, lanes), lanes)

        def widen(i, c):
            part = amp_own[pl.ds(i * block, block), :, cols].astype(jnp.float32)
            wide[pl.ds(pl.multiple_of(i * block * rows, block * rows), block * rows), :] = part.reshape(block * rows, lanes)
            return c

        lax.fori_loop(0, total // block, widen, 0)

        def one_row(a, c):
            sel = pl.ds(a, total, stride=rows)
            value = wide[sel, :].astype(jnp.bfloat16)
            wide[sel, :] = jnp.dot(ladder_v[...], value, preferred_element_type=jnp.float32)
            return c

        lax.fori_loop(0, rows, one_row, 0)

        def narrow(i, c):
            part = wide[pl.ds(pl.multiple_of(i * block * rows, block * rows), block * rows), :].astype(jnp.bfloat16)
            amp_own[pl.ds(i * block, block), :, cols] = part.reshape(block, rows, lanes)
            return c

        lax.fori_loop(0, total // block, narrow, 0)
        return carry

    lax.fori_loop(0, width // lanes, columns, 0)
    store_hole = pltpu.make_async_copy(amp_own, own_hole, local_sem.at[0])
    store_hole.start()
    store_hole.wait()

    hole_copies = []
    for k in order:
        dest = me ^ k
        copy = pltpu.make_async_remote_copy(
            own_hole.at[pl.ds(dest * pairs, pairs)], hole_all.at[:, mine],
            hole_send.at[k], hole_recv.at[k], device_id={"pair": dest}, device_id_type=MESH,
        )
        copy.start()
        hole_copies.append(copy)
    keep_hole = pltpu.make_async_copy(own_hole.at[own_pairs], hole_all.at[:, mine], local_sem.at[1])
    keep_hole.start()

    load_ids.wait()
    load_occ.wait()
    load_vir.wait()

    def add_virtuals(i, carry):
        at = pl.ds(pl.multiple_of(i * lanes, lanes), lanes)
        row = vir_v[:, at]
        diagonal = lax.broadcasted_iota(jnp.int32, (lanes, lanes), 0) == lax.broadcasted_iota(jnp.int32, (lanes, lanes), 1)
        column = jnp.sum(jnp.where(diagonal, row, 0.0), axis=1, keepdims=True)
        vir_sum[at, :] = column + vir_v[...]
        return carry

    lax.fori_loop(0, full // lanes, add_virtuals, 0)

    load_chol.wait()
    keep_amp.wait()
    for copy in amp_copies:
        copy.wait_recv()

    def one_pair(p, carry):
        result[p] = jnp.zeros((full, full), jnp.float32)

        def one_vector(q, c):
            vector = chol_v[q]
            mixed = jnp.dot(vector, amp_all[p], preferred_element_type=jnp.float32).astype(jnp.bfloat16)
            result[p] += lax.dot_general(
                mixed, vector, (((1,), (1,)), ((), ())), preferred_element_type=jnp.float32
            )
            return c

        lax.fori_loop(0, n_vec, one_vector, 0)
        return carry

    lax.fori_loop(0, pairs, one_pair, 0)

    def finish(k):
        source = me ^ k
        at = pl.ds(pl.multiple_of(source * rows, rows), rows)

        def one(p, carry):
            pair = ids_s[p]
            shift = occ_s[pair // NO] + occ_s[pair % NO]
            value = hole_all[p, at, :].astype(jnp.float32) + result[p, at, :]
            result[p, at, :] = value / (vir_sum[at, :] - shift)
            return carry

        lax.fori_loop(0, pairs, one, 0)
        put = pltpu.make_async_copy(result.at[:, at], out.at[:, at], out_sem.at[k])
        put.start()
        return put

    keep_hole.wait()
    puts = [finish(0)]
    for k, copy in zip(order, hole_copies):
        copy.wait_recv()
        puts.append(finish(k))
    for copy in amp_copies:
        copy.wait_send()
    for copy in hole_copies:
        copy.wait_send()
    for put in puts:
        put.wait()


def exchange_and_contract(amplitudes, ladder, cholesky, pair_ids, occ_energy, vir_energy):
    n = lax.axis_size("pair")
    total, rows, width = amplitudes.shape
    pairs = total // n
    full = rows * n
    anywhere = pl.BlockSpec(memory_space=pl.ANY)
    result, _ = pl.pallas_call(
        functools.partial(residual_kernel, n),
        out_shape=[
            jax.ShapeDtypeStruct((pairs, full, full), jnp.float32),
            jax.ShapeDtypeStruct(amplitudes.shape, jnp.bfloat16),
        ],
        in_specs=[anywhere] * 6,
        out_specs=[anywhere, anywhere],
        scratch_shapes=[
            pltpu.VMEM(amplitudes.shape, jnp.bfloat16),
            pltpu.VMEM((total * rows, 128), jnp.float32),
            pltpu.VMEM(ladder.shape, jnp.bfloat16),
            pltpu.VMEM(cholesky.shape, jnp.bfloat16),
            pltpu.VMEM((pairs, full, width), jnp.bfloat16),
            pltpu.VMEM((pairs, full, width), jnp.bfloat16),
            pltpu.VMEM((full, full), jnp.float32),
            pltpu.VMEM((1, full), jnp.float32),
            pltpu.VMEM((pairs, full, full), jnp.float32),
            pltpu.SMEM(pair_ids.shape, jnp.int32),
            pltpu.SMEM(occ_energy.shape, jnp.float32),
            pltpu.SemaphoreType.DMA((n,)),
            pltpu.SemaphoreType.DMA((n,)),
            pltpu.SemaphoreType.DMA((n,)),
            pltpu.SemaphoreType.DMA((n,)),
            pltpu.SemaphoreType.DMA((7,)),
            pltpu.SemaphoreType.DMA((n,)),
        ],
        compiler_params=pltpu.CompilerParams(
            collective_id=0, has_side_effects=True, vmem_limit_bytes=60 * 1024 * 1024
        ),
    )(amplitudes, ladder, cholesky, pair_ids, occ_energy, vir_energy.reshape(1, -1))
    return result


def exchange_plain(amplitudes, ladder, cholesky):
    flat = amplitudes.reshape(amplitudes.shape[0], -1)
    hole = jnp.dot(ladder, flat, preferred_element_type=jnp.float32).astype(jnp.bfloat16)
    hole = hole.reshape(amplitudes.shape)
    pair_amps = lax.all_to_all(amplitudes, "pair", split_axis=0, concat_axis=1, tiled=True)
    pair_hole = lax.all_to_all(hole, "pair", split_axis=0, concat_axis=1, tiled=True)
    mixed = jnp.einsum(
        "qac,pcd->qpad", cholesky, pair_amps, preferred_element_type=jnp.float32
    ).astype(jnp.bfloat16)
    particle = jnp.einsum("qpad,qbd->pab", mixed, cholesky, preferred_element_type=jnp.float32)
    return pair_hole, particle


def shards(amplitudes, ladder, cholesky, pair_ids, occ_energy, vir_energy):
    n = lax.axis_size("pair")
    n_aux = lax.axis_size("aux")
    half_width = amplitudes.shape[2] // n_aux
    aux_index = lax.axis_index("aux")
    aligned = amplitudes.shape[1] % 16 == 0 and n & (n - 1) == 0 and n >= 4
    if aligned and n_aux == 1:
        return exchange_and_contract(amplitudes, ladder, cholesky, pair_ids, occ_energy, vir_energy)
    hole, particle = exchange_plain(amplitudes, ladder, cholesky)
    if n_aux > 1:
        hole = lax.dynamic_slice_in_dim(hole, aux_index * half_width, half_width, 2)
        particle = lax.psum_scatter(particle, "aux", scatter_dimension=2, tiled=True)
    orbitals = jnp.arange(NO, dtype=jnp.int32)
    first_hot = (pair_ids // NO)[:, None] == orbitals[None, :]
    second_hot = (pair_ids % NO)[:, None] == orbitals[None, :]
    hot = first_hot.astype(jnp.float32) + second_hot.astype(jnp.float32)
    occ_sum = jnp.sum(hot * occ_energy[None, :], axis=1)
    vir_cols = lax.dynamic_slice_in_dim(vir_energy, aux_index * half_width, half_width, 0)
    denominator = vir_energy[None, :, None] + vir_cols[None, None, :] - occ_sum[:, None, None]
    return (hole.astype(jnp.float32) + particle) / denominator


def solution(mesh):
    in_specs = (P(None, "pair", None), P(), P("aux", None, None), P("pair"), P(), P())
    out_specs = P("pair", None, "aux")
    return jax.shard_map(shards, mesh=mesh, in_specs=in_specs, out_specs=out_specs, check_vma=False)
```

profile of v0, /device:TPU:0, one launch (start us, length us, event | category | flops | bytes accessed | tf_op | source)
XLA Modules:
  0.0 203.1 jit_solution(3257781046889137259)
XLA Ops:
  0.0 195.3 %shard_map.64 = (f32[8,512,512]{2,1,0:T(8,128)}, bf16[256,16,512]{2,1,0:T(8,128)(2,1)}) custom-call(bf16[256,16,512]{2,1,0:T(8,128)(2,1)} %amps.1, bf16[256,256]{1,0:T(8,128)(2,1)} %ladder.1, bf16[8,512,512]{2,1,0:T(8,128)(2,1)} %chol.1, s32[8]{0:T(128)} %pair_ids.1, f32[16]{0:T(128)} %occ.1, f32[1,512]{1,0:T(1,128)} %bitcast.1), custom_call_target="tpu_custom_call" | custom-call | tf_op jit(solution)/shard_map/pallas_call | solution.py:177
  195.3 7.8 %copy.8 = f32[8,512,512]{2,1,0:T(8,128)} copy(f32[8,512,512]{2,1,0:T(8,128)} %get-tuple-element.6) | data formatting | bytes 16777216
where the time goes:
time: 203 us
  Pallas kernels  195 us (96%)
  local copies, waits for them, and re-layouts  7.76 us (4%)
    pallas_call x1, Pallas kernels, exchange_and_contract(): pl.pallas_call(functools.partial(residual_kernel, n), out_shape=[jax.Shap...  195 us
    unnamed x1, local copies, waits for them, and re-layouts  7.76 us

commit v1 on v0

--- a/solution.py
+++ b/solution.py
@@ -8,23 +8,56 @@
 from jax.sharding import PartitionSpec as P
 
 NO = 16
+VMEM_BYTES = 67043328
 MESH = pl.DeviceIdType.MESH
 
 
+def by_core(core, even, odd):
+    return even + core * (odd - even)
+
+
+def send_orders(n):
+    half, quarter = n // 2, n // 4
+    crossing = [a + b for a in range(quarter) for b in (half + quarter, half)]
+    staying = [a + b for a in range(quarter) for b in (quarter, 0) if a + b]
+    return crossing, staying
+
+
+def arrival_order(first, second):
+    return [k for k in first if k % 2 == 0] + [k for k in second if k % 2], [k for k in second if k % 2 == 0] + [k for k in first if k % 2]
+
+
 def residual_kernel(
-    n, amps, ladder, chol, pair_ids, occ, vir, out, own_hole,
-    amp_own, wide, ladder_v, chol_v, amp_all, hole_all, vir_sum, vir_v, result, ids_s, occ_s,
-    amp_send, amp_recv, hole_send, hole_recv, local_sem, out_sem,
+    n, amps, ladder, chol, pair_ids, occ, vir, result, own_hole,
+    amp_own, wide, ladder_v, chol_v, amp_all, hole_all, vir_sum, vir_v, ids_s, occ_s,
+    amp_send, amp_recv, hole_send, hole_recv, local_sem,
 ):
     total, rows, width = amps.shape
     pairs = total // n
     full = rows * n
     n_vec = chol.shape[0]
     me = lax.axis_index("pair")
-    half, quarter = n // 2, n // 4
-    order = [a + b for a in range(quarter) for b in (half + quarter, half, quarter, 0) if a + b]
+    core = me % 2
+    crossing, staying = send_orders(n)
     mine = pl.ds(pl.multiple_of(me * rows, rows), rows)
     own_pairs = pl.ds(me * pairs, pairs)
+
+    def rows_of(source):
+        return pl.ds(pl.multiple_of(source * rows, rows), rows)
+
+    def amp_copy(k):
+        dest = me ^ k
+        return pltpu.make_async_remote_copy(
+            amps.at[pl.ds(dest * pairs, pairs)], amp_all.at[:, mine],
+            amp_send.at[k], amp_recv.at[k], device_id={"pair": dest}, device_id_type=MESH,
+        )
+
+    def hole_copy(k):
+        dest = me ^ k
+        return pltpu.make_async_remote_copy(
+            own_hole.at[pl.ds(dest * pairs, pairs)], hole_all.at[:, mine],
+            hole_send.at[k], hole_recv.at[k], device_id={"pair": dest}, device_id_type=MESH,
+        )
 
     load_amp = pltpu.make_async_copy(amps, amp_own, local_sem.at[0])
     load_ladder = pltpu.make_async_copy(ladder, ladder_v, local_sem.at[1])
@@ -39,15 +72,8 @@
         pl.semaphore_signal(barrier, inc=1, device_id={"pair": me ^ k}, device_id_type=MESH)
     pl.semaphore_wait(barrier, n - 1)
 
-    amp_copies = []
-    for k in order:
-        dest = me ^ k
-        copy = pltpu.make_async_remote_copy(
-            amps.at[pl.ds(dest * pairs, pairs)], amp_all.at[:, mine],
-            amp_send.at[k], amp_recv.at[k], device_id={"pair": dest}, device_id_type=MESH,
-        )
-        copy.start()
-        amp_copies.append(copy)
+    for even, odd in zip(crossing + staying, staying + crossing):
+        amp_copy(by_core(core, even, odd)).start()
     load_amp.start()
     load_ladder.start()
     load_chol.start()
@@ -92,15 +118,8 @@
     store_hole.start()
     store_hole.wait()
 
-    hole_copies = []
-    for k in order:
-        dest = me ^ k
-        copy = pltpu.make_async_remote_copy(
-            own_hole.at[pl.ds(dest * pairs, pairs)], hole_all.at[:, mine],
-            hole_send.at[k], hole_recv.at[k], device_id={"pair": dest}, device_id_type=MESH,
-        )
-        copy.start()
-        hole_copies.append(copy)
+    for even, odd in zip(staying + crossing, crossing + staying):
+        hole_copy(by_core(core, even, odd)).start()
     keep_hole = pltpu.make_async_copy(own_hole.at[own_pairs], hole_all.at[:, mine], local_sem.at[1])
     keep_hole.start()
 
@@ -120,8 +139,8 @@
 
     load_chol.wait()
     keep_amp.wait()
-    for copy in amp_copies:
-        copy.wait_recv()
+    for k in range(1, n):
+        amp_copy(k).wait_recv()
 
     def one_pair(p, carry):
         result[p] = jnp.zeros((full, full), jnp.float32)
@@ -140,8 +159,7 @@
     lax.fori_loop(0, pairs, one_pair, 0)
 
     def finish(k):
-        source = me ^ k
-        at = pl.ds(pl.multiple_of(source * rows, rows), rows)
+        at = rows_of(me ^ k)
 
         def one(p, carry):
             pair = ids_s[p]
@@ -151,19 +169,28 @@
             return carry
 
         lax.fori_loop(0, pairs, one, 0)
-        put = pltpu.make_async_copy(result.at[:, at], out.at[:, at], out_sem.at[k])
+
+    keep_hole.wait()
+    finish(0)
+    early, late = arrival_order(staying, crossing)
+    for even, odd in zip(early + late, late + early):
+        k = by_core(core, even, odd)
+        hole_copy(k).wait_recv()
+        finish(k)
+    for k in range(1, n):
+        amp_copy(k).wait_send()
+        hole_copy(k).wait_send()
+
+
+def write_kernel(result, out, sems):
+    pieces = sems.shape[0]
+    size = result.shape[0] // pieces
+    puts = [
+        pltpu.make_async_copy(result.at[pl.ds(i * size, size)], out.at[pl.ds(i * size, size)], sems.at[i])
+        for i in range(pieces)
+    ]
+    for put in puts:
         put.start()
-        return put
-
-    keep_hole.wait()
-    puts = [finish(0)]
-    for k, copy in zip(order, hole_copies):
-        copy.wait_recv()
-        puts.append(finish(k))
-    for copy in amp_copies:
-        copy.wait_send()
-    for copy in hole_copies:
-        copy.wait_send()
     for put in puts:
         put.wait()
 
@@ -174,14 +201,16 @@
     pairs = total // n
     full = rows * n
     anywhere = pl.BlockSpec(memory_space=pl.ANY)
+    in_hbm = pl.BlockSpec(memory_space=pltpu.HBM)
+    in_vmem = pl.BlockSpec(memory_space=pltpu.VMEM)
     result, _ = pl.pallas_call(
         functools.partial(residual_kernel, n),
         out_shape=[
-            jax.ShapeDtypeStruct((pairs, full, full), jnp.float32),
+            pltpu.VMEM((pairs, full, full), jnp.float32),
             jax.ShapeDtypeStruct(amplitudes.shape, jnp.bfloat16),
         ],
-        in_specs=[anywhere] * 6,
-        out_specs=[anywhere, anywhere],
+        in_specs=[in_hbm] * 6,
+        out_specs=[in_vmem, in_hbm],
         scratch_shapes=[
             pltpu.VMEM(amplitudes.shape, jnp.bfloat16),
             pltpu.VMEM((total * rows, 128), jnp.float32),
@@ -191,7 +220,6 @@
             pltpu.VMEM((pairs, full, width), jnp.bfloat16),
             pltpu.VMEM((full, full), jnp.float32),
             pltpu.VMEM((1, full), jnp.float32),
-            pltpu.VMEM((pairs, full, full), jnp.float32),
             pltpu.SMEM(pair_ids.shape, jnp.int32),
             pltpu.SMEM(occ_energy.shape, jnp.float32),
             pltpu.SemaphoreType.DMA((n,)),
@@ -199,13 +227,19 @@
             pltpu.SemaphoreType.DMA((n,)),
             pltpu.SemaphoreType.DMA((n,)),
             pltpu.SemaphoreType.DMA((7,)),
-            pltpu.SemaphoreType.DMA((n,)),
         ],
         compiler_params=pltpu.CompilerParams(
-            collective_id=0, has_side_effects=True, vmem_limit_bytes=60 * 1024 * 1024
+            collective_id=0, has_side_effects=True, vmem_limit_bytes=VMEM_BYTES - 4 * pairs * full * full
         ),
     )(amplitudes, ladder, cholesky, pair_ids, occ_energy, vir_energy.reshape(1, -1))
-    return result
+    return pl.pallas_call(
+        write_kernel,
+        out_shape=jax.ShapeDtypeStruct((pairs, full, full), jnp.float32),
+        in_specs=[in_vmem],
+        out_specs=in_hbm,
+        scratch_shapes=[pltpu.SemaphoreType.DMA((pairs,))],
+        compiler_params=pltpu.CompilerParams(vmem_limit_bytes=8 * 1024 * 1024),
+    )(result)
 
 
 def exchange_plain(amplitudes, ladder, cholesky):

time: 203 us -> 201 us (level)
  local copies, waits for them, and re-layouts: 7.76 us -> 0 us
  Pallas kernels: 195 us -> 199 us
    unnamed x1 -> x0, local copies, waits for them, and re-layouts: 7.76 us -> none
    pallas_call x1 -> x2, Pallas kernels: 195 us -> 199 us  [the longest x1 196 us: exchange_and_contract(): pl.pallas_call(functools.partial(residual_kernel, n), out_shape=[pltpu.VM...]
where the time goes in v1:
time: 201 us; the launch traced here: 199 us
  Pallas kernels  199 us (99%)
    pallas_call x1, Pallas kernels, exchange_and_contract(): pl.pallas_call(functools.partial(residual_kernel, n), out_shape=[pltpu.VM...  196 us

profile of v1, /device:TPU:0, one launch (start us, length us, event | category | flops | bytes accessed | tf_op | source)
XLA Modules:
  0.0 199.4 jit_solution(16057752237045421638)
XLA Ops:
  0.0 196.0 %shard_map.64 = (f32[8,512,512]{2,1,0:T(8,128)S(1)}, bf16[256,16,512]{2,1,0:T(8,128)(2,1)}) custom-call(bf16[256,16,512]{2,1,0:T(8,128)(2,1)} %amps.1, bf16[256,256]{1,0:T(8,128)(2,1)} %ladder.1, bf16[8,512,512]{2,1,0:T(8,128)(2,1)} %chol.1, s32[8]{0:T(128)} %pair_ids.1, f32[16]{0:T(128)} %occ.1, f32[1,512]{1,0:T(1,128)} %bitcast.1), custom_call_target="tpu_custom_call" | custom-call | tf_op jit(solution)/shard_map/pallas_call | solution.py:206
  196.0 3.4 %shard_map.65 = f32[8,512,512]{2,1,0:T(8,128)} custom-call(f32[8,512,512]{2,1,0:T(8,128)S(1)} %get-tuple-element.6.result), custom_call_target="tpu_custom_call" | custom-call | tf_op jit(solution)/shard_map/pallas_call | solution.py:235

commit v2 on v1

--- a/solution.py
+++ b/solution.py
@@ -9,6 +9,8 @@
 
 NO = 16
 VMEM_BYTES = 67043328
+LAST = 4
+STEP = 4
 MESH = pl.DeviceIdType.MESH
 
 
@@ -23,13 +25,17 @@
     return crossing, staying
 
 
-def arrival_order(first, second):
-    return [k for k in first if k % 2 == 0] + [k for k in second if k % 2], [k for k in second if k % 2 == 0] + [k for k in first if k % 2]
+def arrival_orders(crossing, staying):
+    cross = [k for k in crossing if k % 2 == 0], [k for k in crossing if k % 2]
+    stay = [k for k in staying if k % 2 == 0], [k for k in staying if k % 2]
+    amps = cross[0] + stay[1] + stay[0] + cross[1], stay[0] + cross[1] + stay[1] + cross[0]
+    holes = stay[0] + cross[1] + stay[1] + cross[0], stay[1] + cross[0] + stay[0] + cross[1]
+    return amps, holes
 
 
 def residual_kernel(
     n, amps, ladder, chol, pair_ids, occ, vir, result, own_hole,
-    amp_own, wide, ladder_v, chol_v, amp_all, hole_all, vir_sum, vir_v, ids_s, occ_s,
+    amp_own, wide, ladder_v, chol_v, amp_all, hole_all, inverse, vir_v, ids_s, occ_s,
     amp_send, amp_recv, hole_send, hole_recv, local_sem,
 ):
     total, rows, width = amps.shape
@@ -118,29 +124,45 @@
     store_hole.start()
     store_hole.wait()
 
-    for even, odd in zip(staying + crossing, crossing + staying):
-        hole_copy(by_core(core, even, odd)).start()
-    keep_hole = pltpu.make_async_copy(own_hole.at[own_pairs], hole_all.at[:, mine], local_sem.at[1])
-    keep_hole.start()
-
     load_ids.wait()
     load_occ.wait()
     load_vir.wait()
 
-    def add_virtuals(i, carry):
-        at = pl.ds(pl.multiple_of(i * lanes, lanes), lanes)
-        row = vir_v[:, at]
-        diagonal = lax.broadcasted_iota(jnp.int32, (lanes, lanes), 0) == lax.broadcasted_iota(jnp.int32, (lanes, lanes), 1)
-        column = jnp.sum(jnp.where(diagonal, row, 0.0), axis=1, keepdims=True)
-        vir_sum[at, :] = column + vir_v[...]
+    def one_inverse(p, carry):
+        pair = ids_s[p]
+        shift = occ_s[pair // NO] + occ_s[pair % NO]
+
+        def add_virtuals(i, c):
+            at = pl.ds(pl.multiple_of(i * lanes, lanes), lanes)
+            row = vir_v[:, at]
+            diagonal = lax.broadcasted_iota(jnp.int32, (lanes, lanes), 0) == lax.broadcasted_iota(jnp.int32, (lanes, lanes), 1)
+            column = jnp.sum(jnp.where(diagonal, row, 0.0), axis=1, keepdims=True)
+            inverse[p, at, :] = 1.0 / (column + vir_v[...] - shift)
+            return c
+
+        lax.fori_loop(0, full // lanes, add_virtuals, 0)
         return carry
 
-    lax.fori_loop(0, full // lanes, add_virtuals, 0)
+    lax.fori_loop(0, pairs, one_inverse, 0)
+
+    amp_order, hole_order = arrival_orders(crossing, staying)
+    arrived = [by_core(core, even, odd) for even, odd in zip(*amp_order)]
+    sent = [by_core(core, even, odd) for even, odd in zip(staying + crossing, crossing + staying)]
+    for k in sent[:len(staying)]:
+        amp_copy(k).wait_send()
+        hole_copy(k).start()
+    for k in arrived[:-LAST]:
+        amp_copy(k).wait_recv()
+    for i, k in enumerate(sent[len(staying):]):
+        amp_copy(k).wait_send()
+        hole_copy(k).start()
+        if STEP <= i + 1 < STEP + LAST:
+            amp_copy(arrived[i + 1 - STEP - LAST]).wait_recv()
+    keep_hole = pltpu.make_async_copy(own_hole.at[own_pairs], hole_all.at[:, mine], local_sem.at[1])
+    keep_hole.start()
 
     load_chol.wait()
     keep_amp.wait()
-    for k in range(1, n):
-        amp_copy(k).wait_recv()
 
     def one_pair(p, carry):
         result[p] = jnp.zeros((full, full), jnp.float32)
@@ -162,23 +184,18 @@
         at = rows_of(me ^ k)
 
         def one(p, carry):
-            pair = ids_s[p]
-            shift = occ_s[pair // NO] + occ_s[pair % NO]
-            value = hole_all[p, at, :].astype(jnp.float32) + result[p, at, :]
-            result[p, at, :] = value / (vir_sum[at, :] - shift)
+            result[p, at, :] = (hole_all[p, at, :].astype(jnp.float32) + result[p, at, :]) * inverse[p, at, :]
             return carry
 
         lax.fori_loop(0, pairs, one, 0)
 
     keep_hole.wait()
     finish(0)
-    early, late = arrival_order(staying, crossing)
-    for even, odd in zip(early + late, late + early):
+    for even, odd in zip(*hole_order):
         k = by_core(core, even, odd)
         hole_copy(k).wait_recv()
         finish(k)
     for k in range(1, n):
-        amp_copy(k).wait_send()
         hole_copy(k).wait_send()
 
 
@@ -218,7 +235,7 @@
             pltpu.VMEM(cholesky.shape, jnp.bfloat16),
             pltpu.VMEM((pairs, full, width), jnp.bfloat16),
             pltpu.VMEM((pairs, full, width), jnp.bfloat16),
-            pltpu.VMEM((full, full), jnp.float32),
+            pltpu.VMEM((pairs, full, full), jnp.float32),
             pltpu.VMEM((1, full), jnp.float32),
             pltpu.SMEM(pair_ids.shape, jnp.int32),
             pltpu.SMEM(occ_energy.shape, jnp.float32),

time: 201 us -> 195 us (0.970)
  Pallas kernels: 199 us -> 195 us
    pallas_call x1, Pallas kernels: 196 us -> 192 us  [exchange_and_contract(): pl.pallas_call(functools.partial(residual_kernel, n), out_shape=[pltpu.VM...]
where the time goes in v2:
time: 195 us
  Pallas kernels  195 us (100%)
    pallas_call x1, Pallas kernels, exchange_and_contract(): pl.pallas_call(functools.partial(residual_kernel, n), out_shape=[pltpu.VM...  192 us

profile of v2, /device:TPU:0, one launch (start us, length us, event | category | flops | bytes accessed | tf_op | source)
XLA Modules:
  0.0 195.2 jit_solution(5691841842865377043)
XLA Ops:
  0.0 191.8 %shard_map.64 = (f32[8,512,512]{2,1,0:T(8,128)S(1)}, bf16[256,16,512]{2,1,0:T(8,128)(2,1)}) custom-call(bf16[256,16,512]{2,1,0:T(8,128)(2,1)} %amps.1, bf16[256,256]{1,0:T(8,128)(2,1)} %ladder.1, bf16[8,512,512]{2,1,0:T(8,128)(2,1)} %chol.1, s32[8]{0:T(128)} %pair_ids.1, f32[16]{0:T(128)} %occ.1, f32[1,512]{1,0:T(1,128)} %bitcast.1), custom_call_target="tpu_custom_call" | custom-call | tf_op jit(solution)/shard_map/pallas_call | solution.py:223
  191.8 3.4 %shard_map.65 = f32[8,512,512]{2,1,0:T(8,128)} custom-call(f32[8,512,512]{2,1,0:T(8,128)S(1)} %get-tuple-element.6.result), custom_call_target="tpu_custom_call" | custom-call | tf_op jit(solution)/shard_map/pallas_call | solution.py:252

commit v3 on v2

--- a/solution.py
+++ b/solution.py
@@ -18,14 +18,22 @@
     return even + core * (odd - even)
 
 
-def send_orders(n):
+def send_orders(n, mid):
+    half, quarter = n // 2, n // 4
+    near = [half + quarter * mid + a for a in range(quarter)]
+    far = [half + quarter * (1 - mid) + a for a in range(quarter)]
+    lead = quarter // 4
+    mixed = [k for pair in zip(far, near[lead:]) for k in pair]
+    outward = near[:lead] + mixed + far[quarter - lead:]
+    mixed = [k for pair in zip(near, far[lead:]) for k in pair]
+    inward = far[:lead] + mixed + near[quarter - lead:]
+    staying = [a + b for a in range(quarter) for b in (quarter, 0) if a + b]
+    return outward, inward, staying
+
+
+def arrival_orders(n, staying):
     half, quarter = n // 2, n // 4
     crossing = [a + b for a in range(quarter) for b in (half + quarter, half)]
-    staying = [a + b for a in range(quarter) for b in (quarter, 0) if a + b]
-    return crossing, staying
-
-
-def arrival_orders(crossing, staying):
     cross = [k for k in crossing if k % 2 == 0], [k for k in crossing if k % 2]
     stay = [k for k in staying if k % 2 == 0], [k for k in staying if k % 2]
     amps = cross[0] + stay[1] + stay[0] + cross[1], stay[0] + cross[1] + stay[1] + cross[0]
@@ -36,7 +44,7 @@
 def residual_kernel(
     n, amps, ladder, chol, pair_ids, occ, vir, result, own_hole,
     amp_own, wide, ladder_v, chol_v, amp_all, hole_all, inverse, vir_v, ids_s, occ_s,
-    amp_send, amp_recv, hole_send, hole_recv, local_sem,
+    amp_send, amp_recv, hole_send, hole_recv, local_sem, entry_sem,
 ):
     total, rows, width = amps.shape
     pairs = total // n
@@ -44,7 +52,9 @@
     n_vec = chol.shape[0]
     me = lax.axis_index("pair")
     core = me % 2
-    crossing, staying = send_orders(n)
+    half, quarter = n // 2, n // 4
+    mid = (me // quarter + 1) // 2 % 2
+    outward, inward, staying = send_orders(n, mid)
     mine = pl.ds(pl.multiple_of(me * rows, rows), rows)
     own_pairs = pl.ds(me * pairs, pairs)
 
@@ -73,13 +83,24 @@
     load_occ = pltpu.make_async_copy(occ, occ_s, local_sem.at[5])
     load_vir = pltpu.make_async_copy(vir, vir_v, local_sem.at[6])
 
+    def tell(sem, k):
+        pl.semaphore_signal(sem, inc=1, device_id={"pair": me ^ k}, device_id_type=MESH)
+
     barrier = pltpu.get_barrier_semaphore()
-    for k in range(1, n):
-        pl.semaphore_signal(barrier, inc=1, device_id={"pair": me ^ k}, device_id_type=MESH)
-    pl.semaphore_wait(barrier, n - 1)
-
-    for even, odd in zip(crossing + staying, staying + crossing):
-        amp_copy(by_core(core, even, odd)).start()
+    low_bits = [1 << i for i in range(quarter.bit_length() - 1)]
+    across, along, last = range(len(low_bits), len(low_bits) + 3)
+
+    @pl.when(mid == 1)
+    def _():
+        tell(barrier, half + quarter)
+
+    for k in low_bits:
+        tell(barrier, k)
+
+    @pl.when(mid == 1)
+    def _():
+        tell(barrier, quarter)
+
     load_amp.start()
     load_ladder.start()
     load_chol.start()
@@ -88,6 +109,47 @@
     load_occ.start()
     load_vir.start()
 
+    pl.semaphore_wait(barrier, len(low_bits) + 1)
+
+    def start_near(first, last):
+        @pl.when(mid == 1)
+        def _():
+            for a in range(first, last):
+                amp_copy(half + quarter + a).start()
+
+    start_near(0, 1)
+    for i, k in enumerate(low_bits):
+        tell(entry_sem.at[i], k)
+        pl.semaphore_wait(entry_sem.at[i], 1)
+        start_near(k, 2 * k)
+
+    @pl.when(mid == 1)
+    def _():
+        tell(entry_sem.at[across], half + quarter)
+        pl.semaphore_wait(entry_sem.at[across], 2)
+        tell(entry_sem.at[along], half + quarter)
+        tell(entry_sem.at[along], quarter)
+        pl.semaphore_wait(entry_sem.at[along], 1)
+        tell(entry_sem.at[last], quarter)
+
+    @pl.when(mid == 0)
+    def _():
+        tell(entry_sem.at[across], quarter)
+        pl.semaphore_wait(entry_sem.at[along], 1)
+        pl.semaphore_wait(entry_sem.at[last], 1)
+
+    first = [by_core(core, even, odd) for even, odd in zip(outward + staying, staying + outward)]
+
+    @pl.when(mid == 1)
+    def _():
+        for k in [half + a for a in range(quarter)] + staying:
+            amp_copy(k).start()
+
+    @pl.when(mid == 0)
+    def _():
+        for k in first:
+            amp_copy(k).start()
+
     load_amp.wait()
     load_ladder.wait()
     block = 16
@@ -145,9 +207,9 @@
 
     lax.fori_loop(0, pairs, one_inverse, 0)
 
-    amp_order, hole_order = arrival_orders(crossing, staying)
+    amp_order, hole_order = arrival_orders(n, staying)
     arrived = [by_core(core, even, odd) for even, odd in zip(*amp_order)]
-    sent = [by_core(core, even, odd) for even, odd in zip(staying + crossing, crossing + staying)]
+    sent = [by_core(core, even, odd) for even, odd in zip(staying + inward, inward + staying)]
     for k in sent[:len(staying)]:
         amp_copy(k).wait_send()
         hole_copy(k).start()
@@ -244,6 +306,7 @@
             pltpu.SemaphoreType.DMA((n,)),
             pltpu.SemaphoreType.DMA((n,)),
             pltpu.SemaphoreType.DMA((7,)),
+            pltpu.SemaphoreType.REGULAR((n.bit_length(),)),
         ],
         compiler_params=pltpu.CompilerParams(
             collective_id=0, has_side_effects=True, vmem_limit_bytes=VMEM_BYTES - 4 * pairs * full * full

time: 195 us -> 192 us (0.985); the launches traced: 195 us -> 189 us
  Pallas kernels: 195 us -> 188 us
    pallas_call x1, Pallas kernels: 192 us -> 185 us  [exchange_and_contract(): pl.pallas_call(functools.partial(residual_kernel, n), out_shape=[pltpu.VM...]
where the time goes in v3:
time: 192 us; the launch traced here: 189 us
  Pallas kernels  188 us (98%)
    pallas_call x1, Pallas kernels, exchange_and_contract(): pl.pallas_call(functools.partial(residual_kernel, n), out_shape=[pltpu.VM...  185 us

profile of v3, /device:TPU:0, one launch (start us, length us, event | category | flops | bytes accessed | tf_op | source)
XLA Modules:
  0.0 188.5 jit_solution(546091854105469993)
XLA Ops:
  0.0 185.1 %shard_map.64 = (f32[8,512,512]{2,1,0:T(8,128)S(1)}, bf16[256,16,512]{2,1,0:T(8,128)(2,1)}) custom-call(bf16[256,16,512]{2,1,0:T(8,128)(2,1)} %amps.1, bf16[256,256]{1,0:T(8,128)(2,1)} %ladder.1, bf16[8,512,512]{2,1,0:T(8,128)(2,1)} %chol.1, s32[8]{0:T(128)} %pair_ids.1, f32[16]{0:T(128)} %occ.1, f32[1,512]{1,0:T(1,128)} %bitcast.1), custom_call_target="tpu_custom_call" | custom-call | tf_op jit(solution)/shard_map/pallas_call | solution.py:285
  185.1 3.4 %shard_map.65 = f32[8,512,512]{2,1,0:T(8,128)} custom-call(f32[8,512,512]{2,1,0:T(8,128)S(1)} %get-tuple-element.6.result), custom_call_target="tpu_custom_call" | custom-call | tf_op jit(solution)/shard_map/pallas_call | solution.py:315

commit v4 on v3

--- a/solution.py
+++ b/solution.py
@@ -18,25 +18,41 @@
     return even + core * (odd - even)
 
 
-def send_orders(n, mid):
+def weave(first, second):
+    return [k for pair in zip(first, second) for k in pair]
+
+
+def amp_orders(n, mid):
     half, quarter = n // 2, n // 4
+    chip = list(range(1, quarter))
+    beside = [quarter + a for a in range(quarter)]
     near = [half + quarter * mid + a for a in range(quarter)]
     far = [half + quarter * (1 - mid) + a for a in range(quarter)]
     lead = quarter // 4
-    mixed = [k for pair in zip(far, near[lead:]) for k in pair]
-    outward = near[:lead] + mixed + far[quarter - lead:]
-    mixed = [k for pair in zip(near, far[lead:]) for k in pair]
-    inward = far[:lead] + mixed + near[quarter - lead:]
+    outward = near[:lead] + weave(far, near[lead:]) + far[quarter - lead:]
+    outer_order = weave(outward[:quarter], beside) + outward[quarter:] + chip
+    middle_rest = beside + [half + a for a in range(quarter)] + chip
+    return outer_order, middle_rest
+
+
+def hole_orders(n, mid):
+    half, quarter = n // 2, n // 4
+    near = [half + quarter * mid + a for a in reversed(range(quarter))]
+    far = [half + quarter * (1 - mid) + a for a in reversed(range(quarter))]
+    lead = quarter // 4
+    inward = far[:lead] + weave(near, far[lead:]) + near[quarter - lead:]
     staying = [a + b for a in range(quarter) for b in (quarter, 0) if a + b]
-    return outward, inward, staying
-
-
-def arrival_orders(n, staying):
+    return staying + inward, inward + staying
+
+
+def arrival_orders(n):
     half, quarter = n // 2, n // 4
     crossing = [a + b for a in range(quarter) for b in (half + quarter, half)]
+    staying = [a + b for a in range(quarter) for b in (quarter, 0) if a + b]
     cross = [k for k in crossing if k % 2 == 0], [k for k in crossing if k % 2]
     stay = [k for k in staying if k % 2 == 0], [k for k in staying if k % 2]
     amps = cross[0] + stay[1] + stay[0] + cross[1], stay[0] + cross[1] + stay[1] + cross[0]
+    cross = cross[0][::-1], cross[1][::-1]
     holes = stay[0] + cross[1] + stay[1] + cross[0], stay[1] + cross[0] + stay[0] + cross[1]
     return amps, holes
 
@@ -54,7 +70,7 @@
     core = me % 2
     half, quarter = n // 2, n // 4
     mid = (me // quarter + 1) // 2 % 2
-    outward, inward, staying = send_orders(n, mid)
+    outer_order, middle_rest = amp_orders(n, mid)
     mine = pl.ds(pl.multiple_of(me * rows, rows), rows)
     own_pairs = pl.ds(me * pairs, pairs)
 
@@ -138,16 +154,14 @@
         pl.semaphore_wait(entry_sem.at[along], 1)
         pl.semaphore_wait(entry_sem.at[last], 1)
 
-    first = [by_core(core, even, odd) for even, odd in zip(outward + staying, staying + outward)]
-
     @pl.when(mid == 1)
     def _():
-        for k in [half + a for a in range(quarter)] + staying:
+        for k in middle_rest:
             amp_copy(k).start()
 
     @pl.when(mid == 0)
     def _():
-        for k in first:
+        for k in outer_order:
             amp_copy(k).start()
 
     load_amp.wait()
@@ -207,15 +221,16 @@
 
     lax.fori_loop(0, pairs, one_inverse, 0)
 
-    amp_order, hole_order = arrival_orders(n, staying)
+    amp_order, hole_order = arrival_orders(n)
     arrived = [by_core(core, even, odd) for even, odd in zip(*amp_order)]
-    sent = [by_core(core, even, odd) for even, odd in zip(staying + inward, inward + staying)]
-    for k in sent[:len(staying)]:
+    sent = [by_core(core, even, odd) for even, odd in zip(*hole_orders(n, mid))]
+    staying = half - 1
+    for k in sent[:staying]:
         amp_copy(k).wait_send()
         hole_copy(k).start()
     for k in arrived[:-LAST]:
         amp_copy(k).wait_recv()
-    for i, k in enumerate(sent[len(staying):]):
+    for i, k in enumerate(sent[staying:]):
         amp_copy(k).wait_send()
         hole_copy(k).start()
         if STEP <= i + 1 < STEP + LAST:

time: 192 us -> 188 us (0.979); the launches traced: 189 us -> 187 us
  no operation moved by 1% of the time
where the time goes in v4:
time: 188 us; the launch traced here: 187 us
  Pallas kernels  187 us (99%)
    pallas_call x1, Pallas kernels, exchange_and_contract(): pl.pallas_call(functools.partial(residual_kernel, n), out_shape=[pltpu.VM...  184 us

profile of v4, /device:TPU:0, one launch (start us, length us, event | category | flops | bytes accessed | tf_op | source)
XLA Modules:
  0.0 186.9 jit_solution(16212069365284179271)
XLA Ops:
  0.0 183.5 %shard_map.64 = (f32[8,512,512]{2,1,0:T(8,128)S(1)}, bf16[256,16,512]{2,1,0:T(8,128)(2,1)}) custom-call(bf16[256,16,512]{2,1,0:T(8,128)(2,1)} %amps.1, bf16[256,256]{1,0:T(8,128)(2,1)} %ladder.1, bf16[8,512,512]{2,1,0:T(8,128)(2,1)} %chol.1, s32[8]{0:T(128)} %pair_ids.1, f32[16]{0:T(128)} %occ.1, f32[1,512]{1,0:T(1,128)} %bitcast.1), custom_call_target="tpu_custom_call" | custom-call | tf_op jit(solution)/shard_map/pallas_call | solution.py:300
  183.5 3.4 %shard_map.65 = f32[8,512,512]{2,1,0:T(8,128)} custom-call(f32[8,512,512]{2,1,0:T(8,128)S(1)} %get-tuple-element.6.result), custom_call_target="tpu_custom_call" | custom-call | tf_op jit(solution)/shard_map/pallas_call | solution.py:330

commit v5 on v4

--- a/solution.py
+++ b/solution.py
@@ -9,8 +9,7 @@
 
 NO = 16
 VMEM_BYTES = 67043328
-LAST = 4
-STEP = 4
+STEP = 8
 MESH = pl.DeviceIdType.MESH
 
 
@@ -45,22 +44,10 @@
     return staying + inward, inward + staying
 
 
-def arrival_orders(n):
-    half, quarter = n // 2, n // 4
-    crossing = [a + b for a in range(quarter) for b in (half + quarter, half)]
-    staying = [a + b for a in range(quarter) for b in (quarter, 0) if a + b]
-    cross = [k for k in crossing if k % 2 == 0], [k for k in crossing if k % 2]
-    stay = [k for k in staying if k % 2 == 0], [k for k in staying if k % 2]
-    amps = cross[0] + stay[1] + stay[0] + cross[1], stay[0] + cross[1] + stay[1] + cross[0]
-    cross = cross[0][::-1], cross[1][::-1]
-    holes = stay[0] + cross[1] + stay[1] + cross[0], stay[1] + cross[0] + stay[0] + cross[1]
-    return amps, holes
-
-
 def residual_kernel(
     n, amps, ladder, chol, pair_ids, occ, vir, result, own_hole,
     amp_own, wide, ladder_v, chol_v, amp_all, hole_all, inverse, vir_v, ids_s, occ_s,
-    amp_send, amp_recv, hole_send, hole_recv, local_sem, entry_sem,
+    send_sem, amp_recv, hole_recv, local_sem, entry_sem,
 ):
     total, rows, width = amps.shape
     pairs = total // n
@@ -79,17 +66,29 @@
 
     def amp_copy(k):
         dest = me ^ k
+        last = k // half * (k % quarter // (quarter // 2)) * core
         return pltpu.make_async_remote_copy(
             amps.at[pl.ds(dest * pairs, pairs)], amp_all.at[:, mine],
-            amp_send.at[k], amp_recv.at[k], device_id={"pair": dest}, device_id_type=MESH,
+            send_sem.at[0], amp_recv.at[last], device_id={"pair": dest}, device_id_type=MESH,
         )
 
     def hole_copy(k):
         dest = me ^ k
+        cross = k // half
+        single = (1 - core) * cross
+        slot = single * (k % quarter // 2 * 2 + k // quarter % 2) + (1 - single) * (quarter + 2 * core + cross)
         return pltpu.make_async_remote_copy(
             own_hole.at[pl.ds(dest * pairs, pairs)], hole_all.at[:, mine],
-            hole_send.at[k], hole_recv.at[k], device_id={"pair": dest}, device_id_type=MESH,
+            send_sem.at[1], hole_recv.at[slot], device_id={"pair": dest}, device_id_type=MESH,
         )
+
+    def wait_blocks(ref, count, sem):
+        part = ref.at[:, pl.ds(0, count * rows)]
+        pltpu.make_async_copy(part, part, sem).wait()
+
+    def wait_sent(ref, sem):
+        part = ref.at[pl.ds(0, (n - 1) * pairs)]
+        pltpu.make_async_copy(part, part, sem).wait()
 
     load_amp = pltpu.make_async_copy(amps, amp_own, local_sem.at[0])
     load_ladder = pltpu.make_async_copy(ladder, ladder_v, local_sem.at[1])
@@ -221,20 +220,16 @@
 
     lax.fori_loop(0, pairs, one_inverse, 0)
 
-    amp_order, hole_order = arrival_orders(n)
-    arrived = [by_core(core, even, odd) for even, odd in zip(*amp_order)]
+    wait_sent(amps, send_sem.at[0])
     sent = [by_core(core, even, odd) for even, odd in zip(*hole_orders(n, mid))]
-    staying = half - 1
-    for k in sent[:staying]:
-        amp_copy(k).wait_send()
+    for k in sent[:half - 1]:
         hole_copy(k).start()
-    for k in arrived[:-LAST]:
-        amp_copy(k).wait_recv()
-    for i, k in enumerate(sent[staying:]):
-        amp_copy(k).wait_send()
+    wait_blocks(amp_all, n - 1 - half // 4, amp_recv.at[0])
+    for k in sent[half - 1:half - 1 + STEP]:
         hole_copy(k).start()
-        if STEP <= i + 1 < STEP + LAST:
-            amp_copy(arrived[i + 1 - STEP - LAST]).wait_recv()
+    wait_blocks(amp_all, half // 4, amp_recv.at[1])
+    for k in sent[half - 1 + STEP:]:
+        hole_copy(k).start()
     keep_hole = pltpu.make_async_copy(own_hole.at[own_pairs], hole_all.at[:, mine], local_sem.at[1])
     keep_hole.start()
 
@@ -267,13 +262,34 @@
         lax.fori_loop(0, pairs, one, 0)
 
     keep_hole.wait()
-    finish(0)
-    for even, odd in zip(*hole_order):
-        k = by_core(core, even, odd)
-        hole_copy(k).wait_recv()
-        finish(k)
-    for k in range(1, n):
-        hole_copy(k).wait_send()
+
+    def finish_some(base):
+        def one(i, carry):
+            finish(base + 2 * i)
+            return carry
+
+        lax.fori_loop(0, half // 2, one, 0)
+
+    def wait_staying(slot, fewer):
+        @pl.when(fewer == 1)
+        def _():
+            wait_blocks(hole_all, half // 2 - 1, hole_recv.at[slot])
+
+        @pl.when(fewer == 0)
+        def _():
+            wait_blocks(hole_all, half // 2, hole_recv.at[slot])
+
+    wait_staying(quarter, 1 - core)
+    finish_some(core)
+    wait_blocks(hole_all, half // 2, hole_recv.at[quarter + 3])
+    finish_some(half + 1 - core)
+    wait_staying(quarter + 2, core)
+    finish_some(1 - core)
+    for a in reversed(range(quarter // 2)):
+        for step in range(2):
+            wait_blocks(hole_all, 1, hole_recv.at[2 * a + step])
+            finish(half + quarter * step + 2 * a + core)
+    wait_sent(own_hole, send_sem.at[1])
 
 
 def write_kernel(result, out, sems):
@@ -316,10 +332,9 @@
             pltpu.VMEM((1, full), jnp.float32),
             pltpu.SMEM(pair_ids.shape, jnp.int32),
             pltpu.SMEM(occ_energy.shape, jnp.float32),
-            pltpu.SemaphoreType.DMA((n,)),
-            pltpu.SemaphoreType.DMA((n,)),
-            pltpu.SemaphoreType.DMA((n,)),
-            pltpu.SemaphoreType.DMA((n,)),
+            pltpu.SemaphoreType.DMA((2,)),
+            pltpu.SemaphoreType.DMA((2,)),
+            pltpu.SemaphoreType.DMA((n // 4 + 4,)),
             pltpu.SemaphoreType.DMA((7,)),
             pltpu.SemaphoreType.REGULAR((n.bit_length(),)),
         ],
@@ -355,7 +370,7 @@
     n_aux = lax.axis_size("aux")
     half_width = amplitudes.shape[2] // n_aux
     aux_index = lax.axis_index("aux")
-    aligned = amplitudes.shape[1] % 16 == 0 and n & (n - 1) == 0 and n >= 4
+    aligned = amplitudes.shape[1] % 16 == 0 and n & (n - 1) == 0 and n >= 16
     if aligned and n_aux == 1:
         return exchange_and_contract(amplitudes, ladder, cholesky, pair_ids, occ_energy, vir_energy)
     hole, particle = exchange_plain(amplitudes, ladder, cholesky)

time: 188 us -> 188 us (level)
  no operation moved by 1% of the time
where the time goes in v5:
time: 188 us; the launch traced here: 186 us
  Pallas kernels  186 us (99%)
    pallas_call x1, Pallas kernels, exchange_and_contract(): pl.pallas_call(functools.partial(residual_kernel, n), out_shape=[pltpu.VM...  182 us

profile of v5, /device:TPU:0, one launch (start us, length us, event | category | flops | bytes accessed | tf_op | source)
XLA Modules:
  0.0 185.9 jit_solution(9068015973210206001)
XLA Ops:
  0.0 182.5 %shard_map.64 = (f32[8,512,512]{2,1,0:T(8,128)S(1)}, bf16[256,16,512]{2,1,0:T(8,128)(2,1)}) custom-call(bf16[256,16,512]{2,1,0:T(8,128)(2,1)} %amps.1, bf16[256,256]{1,0:T(8,128)(2,1)} %ladder.1, bf16[8,512,512]{2,1,0:T(8,128)(2,1)} %chol.1, s32[8]{0:T(128)} %pair_ids.1, f32[16]{0:T(128)} %occ.1, f32[1,512]{1,0:T(1,128)} %bitcast.1), custom_call_target="tpu_custom_call" | custom-call | tf_op jit(solution)/shard_map/pallas_call | solution.py:316
  182.5 3.4 %shard_map.65 = f32[8,512,512]{2,1,0:T(8,128)} custom-call(f32[8,512,512]{2,1,0:T(8,128)S(1)} %get-tuple-element.6.result), custom_call_target="tpu_custom_call" | custom-call | tf_op jit(solution)/shard_map/pallas_call | solution.py:345

commit v6 on v5

--- a/solution.py
+++ b/solution.py
@@ -116,6 +116,45 @@
     def _():
         tell(barrier, quarter)
 
+    pl.semaphore_wait(barrier, len(low_bits) + 1)
+
+    def start_near(first, last):
+        @pl.when(mid == 1)
+        def _():
+            for a in range(first, last):
+                amp_copy(half + quarter + a).start()
+
+    start_near(0, 1)
+    for i, k in enumerate(low_bits):
+        tell(entry_sem.at[i], k)
+        pl.semaphore_wait(entry_sem.at[i], 1)
+        start_near(k, 2 * k)
+
+    @pl.when(mid == 1)
+    def _():
+        tell(entry_sem.at[across], half + quarter)
+        pl.semaphore_wait(entry_sem.at[across], 2)
+        tell(entry_sem.at[along], half + quarter)
+        tell(entry_sem.at[along], quarter)
+        pl.semaphore_wait(entry_sem.at[along], 1)
+        tell(entry_sem.at[last], quarter)
+
+    @pl.when(mid == 0)
+    def _():
+        tell(entry_sem.at[across], quarter)
+        pl.semaphore_wait(entry_sem.at[along], 1)
+        pl.semaphore_wait(entry_sem.at[last], 1)
+
+    @pl.when(mid == 1)
+    def _():
+        for k in middle_rest:
+            amp_copy(k).start()
+
+    @pl.when(mid == 0)
+    def _():
+        for k in outer_order:
+            amp_copy(k).start()
+
     load_amp.start()
     load_ladder.start()
     load_chol.start()
@@ -123,45 +162,6 @@
     load_ids.start()
     load_occ.start()
     load_vir.start()
-
-    pl.semaphore_wait(barrier, len(low_bits) + 1)
-
-    def start_near(first, last):
-        @pl.when(mid == 1)
-        def _():
-            for a in range(first, last):
-                amp_copy(half + quarter + a).start()
-
-    start_near(0, 1)
-    for i, k in enumerate(low_bits):
-        tell(entry_sem.at[i], k)
-        pl.semaphore_wait(entry_sem.at[i], 1)
-        start_near(k, 2 * k)
-
-    @pl.when(mid == 1)
-    def _():
-        tell(entry_sem.at[across], half + quarter)
-        pl.semaphore_wait(entry_sem.at[across], 2)
-        tell(entry_sem.at[along], half + quarter)
-        tell(entry_sem.at[along], quarter)
-        pl.semaphore_wait(entry_sem.at[along], 1)
-        tell(entry_sem.at[last], quarter)
-
-    @pl.when(mid == 0)
-    def _():
-        tell(entry_sem.at[across], quarter)
-        pl.semaphore_wait(entry_sem.at[along], 1)
-        pl.semaphore_wait(entry_sem.at[last], 1)
-
-    @pl.when(mid == 1)
-    def _():
-        for k in middle_rest:
-            amp_copy(k).start()
-
-    @pl.when(mid == 0)
-    def _():
-        for k in outer_order:
-            amp_copy(k).start()
 
     load_amp.wait()
     load_ladder.wait()
@@ -347,7 +347,7 @@
         out_shape=jax.ShapeDtypeStruct((pairs, full, full), jnp.float32),
         in_specs=[in_vmem],
         out_specs=in_hbm,
-        scratch_shapes=[pltpu.SemaphoreType.DMA((pairs,))],
+        scratch_shapes=[pltpu.SemaphoreType.DMA((1,))],
         compiler_params=pltpu.CompilerParams(vmem_limit_bytes=8 * 1024 * 1024),
     )(result)
 

time: 188 us -> 188 us (level)
  no operation moved by 1% of the time
where the time goes in v6:
time: 188 us; the launch traced here: 186 us
  Pallas kernels  186 us (99%)
    pallas_call x1, Pallas kernels, exchange_and_contract(): pl.pallas_call(functools.partial(residual_kernel, n), out_shape=[pltpu.VM...  182 us

profile of v6, /device:TPU:0, one launch (start us, length us, event | category | flops | bytes accessed | tf_op | source)
XLA Modules:
  0.0 185.9 jit_solution(9243859406625344761)
XLA Ops:
  0.0 182.5 %shard_map.64 = (f32[8,512,512]{2,1,0:T(8,128)S(1)}, bf16[256,16,512]{2,1,0:T(8,128)(2,1)}) custom-call(bf16[256,16,512]{2,1,0:T(8,128)(2,1)} %amps.1, bf16[256,256]{1,0:T(8,128)(2,1)} %ladder.1, bf16[8,512,512]{2,1,0:T(8,128)(2,1)} %chol.1, s32[8]{0:T(128)} %pair_ids.1, f32[16]{0:T(128)} %occ.1, f32[1,512]{1,0:T(1,128)} %bitcast.1), custom_call_target="tpu_custom_call" | custom-call | tf_op jit(solution)/shard_map/pallas_call | solution.py:316
  182.5 3.4 %shard_map.65 = f32[8,512,512]{2,1,0:T(8,128)} custom-call(f32[8,512,512]{2,1,0:T(8,128)S(1)} %get-tuple-element.6.result), custom_call_target="tpu_custom_call" | custom-call | tf_op jit(solution)/shard_map/pallas_call | solution.py:345

commit v7 on v5

--- a/solution.py
+++ b/solution.py
@@ -40,6 +40,7 @@
     far = [half + quarter * (1 - mid) + a for a in reversed(range(quarter))]
     lead = quarter // 4
     inward = far[:lead] + weave(near, far[lead:]) + near[quarter - lead:]
+    inward[-1], inward[-2] = inward[-2], inward[-1]
     staying = [a + b for a in range(quarter) for b in (quarter, 0) if a + b]
     return staying + inward, inward + staying
 

time: 188 us -> 188 us (level)
  no operation moved by 1% of the time
where the time goes in v7:
time: 188 us; the launch traced here: 186 us
  Pallas kernels  186 us (99%)
    pallas_call x1, Pallas kernels, exchange_and_contract(): pl.pallas_call(functools.partial(residual_kernel, n), out_shape=[pltpu.VM...  182 us

profile of v7, /device:TPU:0, one launch (start us, length us, event | category | flops | bytes accessed | tf_op | source)
XLA Modules:
  0.0 185.9 jit_solution(10491385822433038877)
XLA Ops:
  0.0 182.5 %shard_map.64 = (f32[8,512,512]{2,1,0:T(8,128)S(1)}, bf16[256,16,512]{2,1,0:T(8,128)(2,1)}) custom-call(bf16[256,16,512]{2,1,0:T(8,128)(2,1)} %amps.1, bf16[256,256]{1,0:T(8,128)(2,1)} %ladder.1, bf16[8,512,512]{2,1,0:T(8,128)(2,1)} %chol.1, s32[8]{0:T(128)} %pair_ids.1, f32[16]{0:T(128)} %occ.1, f32[1,512]{1,0:T(1,128)} %bitcast.1), custom_call_target="tpu_custom_call" | custom-call | tf_op jit(solution)/shard_map/pallas_call | solution.py:317
  182.5 3.4 %shard_map.65 = f32[8,512,512]{2,1,0:T(8,128)} custom-call(f32[8,512,512]{2,1,0:T(8,128)S(1)} %get-tuple-element.6.result), custom_call_target="tpu_custom_call" | custom-call | tf_op jit(solution)/shard_map/pallas_call | solution.py:346

commit v8 on v5

--- a/solution.py
+++ b/solution.py
@@ -290,19 +290,6 @@
             wait_blocks(hole_all, 1, hole_recv.at[2 * a + step])
             finish(half + quarter * step + 2 * a + core)
     wait_sent(own_hole, send_sem.at[1])
-
-
-def write_kernel(result, out, sems):
-    pieces = sems.shape[0]
-    size = result.shape[0] // pieces
-    puts = [
-        pltpu.make_async_copy(result.at[pl.ds(i * size, size)], out.at[pl.ds(i * size, size)], sems.at[i])
-        for i in range(pieces)
-    ]
-    for put in puts:
-        put.start()
-    for put in puts:
-        put.wait()
 
 
 def exchange_and_contract(amplitudes, ladder, cholesky, pair_ids, occ_energy, vir_energy):
@@ -342,14 +329,7 @@
             collective_id=0, has_side_effects=True, vmem_limit_bytes=VMEM_BYTES - 4 * pairs * full * full
         ),
     )(amplitudes, ladder, cholesky, pair_ids, occ_energy, vir_energy.reshape(1, -1))
-    return pl.pallas_call(
-        write_kernel,
-        out_shape=jax.ShapeDtypeStruct((pairs, full, full), jnp.float32),
-        in_specs=[in_vmem],
-        out_specs=in_hbm,
-        scratch_shapes=[pltpu.SemaphoreType.DMA((pairs,))],
-        compiler_params=pltpu.CompilerParams(vmem_limit_bytes=8 * 1024 * 1024),
-    )(result)
+    return result
 
 
 def exchange_plain(amplitudes, ladder, cholesky):

time: 188 us -> 188 us (level)
  Pallas kernels: 186 us -> 182 us
  local copies, waits for them, and re-layouts: 0 us -> 3.4 us
    unnamed x0 -> x1, local copies, waits for them, and re-layouts: none -> 3.4 us
    pallas_call x1 -> x0, Pallas kernels: 3.37 us -> none  [exchange_and_contract(): pl.pallas_call(write_kernel, out_shape=jax.ShapeDtypeStruct((pairs, full,...]
where the time goes in v8:
time: 188 us; the launch traced here: 186 us
  Pallas kernels  182 us (97%)
  local copies, waits for them, and re-layouts  3.4 us (2%)
    pallas_call x1, Pallas kernels, exchange_and_contract(): pl.pallas_call(functools.partial(residual_kernel, n), out_shape=[pltpu.VM...  182 us

profile of v8, /device:TPU:0, one launch (start us, length us, event | category | flops | bytes accessed | tf_op | source)
XLA Modules:
  0.0 185.9 jit_solution(13476151421179317617)
XLA Ops:
  0.0 182.5 %shard_map.64 = (f32[8,512,512]{2,1,0:T(8,128)S(1)}, bf16[256,16,512]{2,1,0:T(8,128)(2,1)}) custom-call(bf16[256,16,512]{2,1,0:T(8,128)(2,1)} %amps.1, bf16[256,256]{1,0:T(8,128)(2,1)} %ladder.1, bf16[8,512,512]{2,1,0:T(8,128)(2,1)} %chol.1, s32[8]{0:T(128)} %pair_ids.1, f32[16]{0:T(128)} %occ.1, f32[1,512]{1,0:T(1,128)} %bitcast.1), custom_call_target="tpu_custom_call" | custom-call | tf_op jit(solution)/shard_map/pallas_call | solution.py:303
  182.5 3.4 %copy.8 = f32[8,512,512]{2,1,0:T(8,128)} copy(f32[8,512,512]{2,1,0:T(8,128)S(1)} %get-tuple-element.6) | data formatting | bytes 16777216
